TPU v7x, 512 devices: a whole 4x4x16 slice. The times are simulated.
512 devices in a mesh: dp: 16 (over x, y_hi, core), expert: 32 (over y_lo, z).
Axes of the slice: x: 4, y: 4 (y_hi: 2, y_lo: 2; y = y_hi * 2 + y_lo), z: 16, core: 2. Of those that a mesh axis runs over, the one named last changes fastest.
Arguments:
- hidden_in: bfloat16 [32, 1024, 2048], P('expert', 'dp'), may hold values from -6 to 6
- queries: bfloat16 [32, 1024, 2048], P('expert', None, 'dp'), may hold values from -150 to 150
- key_pool: bfloat16 [256, 128, 2048], P('expert', None, 'dp'), may hold values from -8 to 8
- value_pool: bfloat16 [256, 128, 2048], P('expert', None, 'dp'), may hold values from -6 to 6
- page_table: int32 [32, 8], P('expert'), may hold values from 0 to 7, as said below
- prompt_lengths: int32 [32, 4], P('expert'), may hold values from 1 to 512, 1024 in all within a row
- expert_ids: int32 [32, 1024, 8], P('expert', 'dp'), may hold values from 0 to 31, all different within a row; in each aligned block of 64 rows (0 to 63, 64 to 127, ..., all dimensions but the last counted through in order) at most 20 rows name the same one
- gate_weights: float32 [32, 1024, 8], P('expert', 'dp'), may hold values from 0.05 to 0.3
- norm_gain: float32 [2048], replicated, may hold values from 0.5 to 1.5
- trainer_gate_up: float32 [32, 2048, 2048], P('expert', 'dp'), may hold values from -0.125 to 0.125
- trainer_down: float32 [32, 1024, 2048], P('expert', 'dp'), may hold values from -0.1875 to 0.1875
Outputs:
- mixed: bfloat16 [32, 1024, 2048], P('expert', 'dp')
Inputs may be any that keep to these rules, and one draw needn't show every extreme that they name: `page_table`: each group's row is a permutation of the group's page numbers. `expert_ids`: among the 64 rows of one device (aligned blocks of rows), no expert is named by more than 20 rows, a bound that some block reaches.
All inputs are finite; a program needn't handle non-finite values.
Results may differ from a plain program's by a relative error of at most 0.0075.
Values may be sent and summed in bfloat16 or wider, within the bound.
A program may use at most 64 MiB of HBM per device.

v0:
```python
import math

import jax
import jax.numpy as jnp
from jax import lax
from jax.sharding import PartitionSpec as P

HDIM = 128
TOPK = 8


epsilon = 1e-05


def fetch_weights(trainer_gate_up, trainer_down):
    return (
        lax.all_gather(trainer_gate_up.astype(jnp.bfloat16), "dp", axis=1, tiled=True),
        lax.all_gather(trainer_down.astype(jnp.bfloat16), "dp", axis=1, tiled=True),
    )


def local(
    hidden_in,
    queries,
    key_pool,
    value_pool,
    page_table,
    prompt_lengths,
    expert_ids,
    gate_weights,
    norm_gain,
    trainer_gate_up,
    trainer_down,
):
    col_tok = queries.shape[1]
    width_dev = queries.shape[2]
    heads_dev = width_dev // HDIM
    keys_all = jnp.take(key_pool, page_table[0], axis=0).reshape(col_tok, heads_dev, HDIM)
    values_all = jnp.take(value_pool, page_table[0], axis=0).reshape(col_tok, heads_dev, HDIM)
    request_ends = jnp.cumsum(prompt_lengths[0])
    positions = lax.iota(jnp.int32, col_tok)
    request = jnp.sum((positions[:, None] >= request_ends[None, :]).astype(jnp.int32), axis=1)
    block_rows = math.gcd(col_tok, 512)
    query_blocks = queries[0].reshape(col_tok // block_rows, block_rows, heads_dev, HDIM)
    request_blocks = request.reshape(col_tok // block_rows, block_rows)
    score_scale = 1.0 / math.sqrt(HDIM)

    def attend(pieces):
        query_block, request_block = pieces
        scores = (
            jnp.einsum("qhd,khd->hqk", query_block, keys_all, preferred_element_type=jnp.float32)
            * score_scale
        )
        same_request = (request_block[:, None] == request[None, :])[None]
        scores = jnp.where(same_request, scores, -1e30)
        highest = jnp.max(scores, axis=-1, keepdims=True)
        weights = jnp.where(same_request, jnp.exp(scores - highest), 0.0)
        totals = jnp.sum(weights, axis=-1, keepdims=True)
        probs = (weights / totals).astype(jnp.bfloat16)
        output = jnp.einsum("hqk,khd->qhd", probs, values_all, preferred_element_type=jnp.float32)
        return output.astype(jnp.bfloat16).reshape(block_rows, width_dev)

    attn_heads = lax.map(attend, (query_blocks, request_blocks)).reshape(1, col_tok, width_dev)
    attn_tokens = lax.all_to_all(attn_heads, "dp", split_axis=1, concat_axis=2, tiled=True)
    resid32 = (
        (hidden_in.astype(jnp.float32) + attn_tokens.astype(jnp.float32))
        .astype(jnp.bfloat16)
        .astype(jnp.float32)
    )
    mean_square = jnp.mean(resid32 * resid32, axis=-1, keepdims=True)
    normed = (resid32 * lax.rsqrt(mean_square + epsilon) * norm_gain).astype(jnp.bfloat16)
    server_gate_up, server_down = fetch_weights(trainer_gate_up, trainer_down)
    token_rows = normed.shape[1]
    width = normed.shape[2]
    expert_count = lax.axis_size("expert")
    capacity = min(token_rows, token_rows * TOPK * 5 // (4 * expert_count))
    hidden_size = server_gate_up.shape[2] // 2
    ids_flat = expert_ids[0].reshape(token_rows * TOPK)
    onehot = (ids_flat[:, None] == lax.iota(jnp.int32, expert_count)[None, :]).astype(jnp.int32)
    earlier = jnp.cumsum(onehot, axis=0) - onehot
    slot_index = jnp.sum(earlier * onehot, axis=1)
    flat_slot = ids_flat * capacity + slot_index
    placement = (
        flat_slot[:, None] == lax.iota(jnp.int32, expert_count * capacity)[None, :]
    ).astype(jnp.bfloat16)
    dispatch_matrix = jnp.sum(placement.reshape(token_rows, TOPK, expert_count * capacity), axis=1)
    outgoing = jnp.einsum(
        "ts,td->sd", dispatch_matrix, normed[0], preferred_element_type=jnp.float32
    )
    outgoing = outgoing.astype(jnp.bfloat16).reshape(expert_count, capacity, width)
    received = lax.all_to_all(outgoing, "expert", split_axis=0, concat_axis=0, tiled=True)
    sources, items, features = received.shape
    slot_rows = received.reshape(sources * items, features)
    gate_up = jnp.dot(slot_rows, server_gate_up[0], preferred_element_type=jnp.float32)
    hidden_units = (jax.nn.silu(gate_up[:, :hidden_size]) * gate_up[:, hidden_size:]).astype(
        jnp.bfloat16
    )
    outputs = jnp.dot(hidden_units, server_down[0], preferred_element_type=jnp.float32).astype(
        jnp.bfloat16
    )
    returned = lax.all_to_all(
        outputs.reshape(sources, items, features), "expert", split_axis=0, concat_axis=0, tiled=True
    )
    copies = jnp.take(returned.reshape(expert_count * capacity, width), flat_slot, axis=0)
    copies = copies.reshape(token_rows, TOPK, width).astype(jnp.float32)
    mixture = jnp.einsum("tk,tkd->td", gate_weights[0], copies)
    mixed = resid32[0] + mixture
    return mixed.astype(jnp.bfloat16)[None]


def solution(mesh):
    placed = (
        P("expert", "dp", None),
        P("expert", None, "dp"),
        P("expert", None, "dp"),
        P("expert", None, "dp"),
        P("expert", None),
        P("expert", None),
        P("expert", "dp", None),
        P("expert", "dp", None),
        P(),
        P("expert", "dp", None),
        P("expert", "dp", None),
    )
    return jax.shard_map(
        local, mesh=mesh, in_specs=placed, out_specs=P("expert", "dp", None), check_vma=False
    )
```

profile of v0, /device:TPU:1, one launch (start us, length us, event | category | flops | bytes accessed | tf_op | source)
XLA Modules:
  0.0 383.2 jit_solution(16259192949662491278)
XLA Ops:
  6.6 2.1 convert_element_type.96
  10.5 4.2 %while.10 = (s32[]{:T(128)}, bf16[2,512,128]{2,1,0:T(8,128)(2,1)S(1)}, s32[2,512]{1,0:T(2,128)S(1)}, s32[1024]{0:T(1024)S(1)}, bf16[2,512,1,128]{3,1,2,0:T(8,128...) while((s32[]{:T(128)}, ...), condition=%wide.region_5.7_spmd, body=%wide.region_2.6_spmd.sunk | while | flops 277412864 | bytes 7110753 | solution.py:63
  11.8 0.8 fusion.56
  13.9 0.8 fusion.56
  15.7 2.2 reduce.8
  17.9 0.8 reshape.245
  18.7 10.2 %all-to-all-start = ((bf16[16,2,4096]{2,1,0:T(2,128)(2,1)}), bf16[16,2,4096]{2,1,0:T(2,128)(2,1)S(1)}, u32[]{:S(2)}, u32[]{:S(2)}) async-start(bf16[16,2,4096]{2,1,0:T(2,128)(2,1)} %reshape.245), calls=%async_computation | async-start | bytes 524288 | tf_op jit(solution)/shard_map/all_to_all | solution.py:64
  29.2 1.2 reduce-window.19
  31.4 6.4 %all-to-all-done = bf16[16,2,4096]{2,1,0:T(2,128)(2,1)S(1)} async-done(((bf16[16,2,4096]{2,1,0:T(2,128)(2,1)}), bf16[16,2,4096]{2,1,0:T(2,128)(2,1)S(1)}, u32[]{:S(2)}, u32[]{:S(2)}) %all-to-all-start) | async-done | bytes 262176 | tf_op jit(solution)/shard_map/all_to_all | solution.py:64
  39.5 0.9 convolution_convert_fusion.1
  40.4 2.4 reshape.206
  42.8 13.5 %all-to-all-start.1 = ((bf16[32,20,2048]{2,1,0:T(8,128)(2,1)}), bf16[32,20,2048]{2,1,0:T(8,128)(2,1)S(1)}, u32[]{:S(2)}, u32[]{:S(2)}) async-start(bf16[32,20,2048]{2,1,0:T(8,128)(2,1)} %reshape.206), calls=%async_computation.1 | async-start | bytes 6291456 | tf_op jit(solution)/shard_map/all_to_all | solution.py:91
  56.6 1.8 convert_element_type.98
  58.4 135.3 %all-to-all-done.1 = bf16[32,20,2048]{2,1,0:T(8,128)(2,1)S(1)} async-done(((bf16[32,20,2048]{2,1,0:T(8,128)(2,1)}), bf16[32,20,2048]{2,1,0:T(8,128)(2,1)S(1)}, u32[]{:S(2)}, u32[]{:S(2)}) %all-to-all-start.1) | async-done | bytes 2621472 | tf_op jit(solution)/shard_map/all_to_all | solution.py:91
  193.7 2.2 reshape.207
  195.9 11.1 %fusion.13 = f32[640,2048]{1,0:T(8,128)} fusion(bf16[640,2048]{1,0:T(8,128)(2,1)} %reshape.207, bf16[1,2048,2048]{2,1,0:T(8,128)(2,1)} %all-gather.3.cloned.1.call-done), kind=kOutput, calls=%fused_computation.21 | convolution fusion | flops 5368709120 | bytes 16252928 | tf_op jit(solution)/shard_map/dot_general | solution.py:94
  207.0 6.7 %fusion.17 = bf16[640,2048]{1,0:T(8,128)(2,1)S(1)} fusion(bf16[1,1024,2048]{2,1,0:T(8,128)(2,1)} %all-gather.5.cloned.1.call-done, f32[640,2048]{1,0:T(8,128)} %fusion.13), kind=kOutput, calls=%fused_computation.26 | convolution fusion | flops 2689597440 | bytes 12058624 | tf_op jit(solution)/shard_map/dot_general | solution.py:98
  213.7 2.4 reshape.208
  216.1 11.8 %all-to-all-start.2 = ((bf16[32,20,2048]{2,1,0:T(8,128)(2,1)}), bf16[32,20,2048]{2,1,0:T(8,128)(2,1)}, u32[]{:S(2)}, u32[]{:S(2)}) async-start(bf16[32,20,2048]{2,1,0:T(8,128)(2,1)} %reshape.208), calls=%async_computation.2 | async-start | bytes 6291456 | tf_op jit(solution)/shard_map/all_to_all | solution.py:101
  228.3 137.8 %all-to-all-done.2 = bf16[32,20,2048]{2,1,0:T(8,128)(2,1)} async-done(((bf16[32,20,2048]{2,1,0:T(8,128)(2,1)}), bf16[32,20,2048]{2,1,0:T(8,128)(2,1)}, u32[]{:S(2)}, u32[]{:S(2)}) %all-to-all-start.2) | async-done | bytes 2621472 | tf_op jit(solution)/shard_map/all_to_all | solution.py:101
  366.0 3.6 reshape.209
  369.7 3.3 gather_fusion
  373.0 2.4 fusion.21
  375.5 0.9 fusion.36
  (72 shorter events, 8.8 us)
Async XLA Ops:
  6.5 2.3 copy-start
  6.5 2.2 copy-start.10
  6.5 2.9 copy-start.3
  6.5 3.5 copy-start.9
  6.5 3.9 %copy-start.8 = (bf16[1,1024,128]{2,1,0:T(8,128)(2,1)S(1)}, bf16[1,1024,128]{2,1,0:T(8,128)(2,1)}, u32[]{:S(2)}) copy-start(bf16[1,1024,128]{2,1,0:T(8,128)(2,1)} %param.16) | copy-start | bytes 786436
  6.5 189.3 %all-gather.3.cloned.1.call-start = ((), (), s32[]{:S(2)}) async-start(), calls=%async_computation.3 | async-start | bytes 8912896 | tf_op jit(solution)/shard_map/all_gather | solution.py:17
  14.7 14.1 %copy-start.5 = (s32[1,64,8]{1,2,0:T(8,128)S(1)}, s32[1,64,8]{1,2,0:T(8,128)}, u32[]{:S(2)}) copy-start(s32[1,64,8]{1,2,0:T(8,128)} %param.21) | copy-start | bytes 6148
  18.7 19.2 %all-to-all-start = ((bf16[16,2,4096]{2,1,0:T(2,128)(2,1)}), bf16[16,2,4096]{2,1,0:T(2,128)(2,1)S(1)}, u32[]{:S(2)}, u32[]{:S(2)}) async-start(bf16[16,2,4096]{2,1,0:T(2,128)(2,1)} %reshape.245), calls=%async_computation | async-start | bytes 524288 | tf_op jit(solution)/shard_map/all_to_all | solution.py:64
  28.9 9.6 %copy-start.4 = (bf16[1,64,2048]{2,1,0:T(8,128)(2,1)S(1)}, bf16[1,64,2048]{2,1,0:T(8,128)(2,1)}, u32[]{:S(2)}) copy-start(bf16[1,64,2048]{2,1,0:T(8,128)(2,1)} %param.15) | copy-start | bytes 786436
  31.4 8.1 %copy-start.6 = (f32[2048]{0:T(1024)S(1)}, f32[2048]{0:T(1024)}, u32[]{:S(2)}) copy-start(f32[2048]{0:T(1024)} %param.23) | copy-start | bytes 24580
  38.8 0.7 copy-start.1
  42.8 150.8 %all-to-all-start.1 = ((bf16[32,20,2048]{2,1,0:T(8,128)(2,1)}), bf16[32,20,2048]{2,1,0:T(8,128)(2,1)S(1)}, u32[]{:S(2)}, u32[]{:S(2)}) async-start(bf16[32,20,2048]{2,1,0:T(8,128)(2,1)} %reshape.206), calls=%async_computation.1 | async-start | bytes 6291456 | tf_op jit(solution)/shard_map/all_to_all | solution.py:91
  56.3 150.7 %all-gather.5.cloned.1.call-start = ((), (), s32[]{:S(2)}) async-start(), calls=%async_computation.4 | async-start | bytes 4456448 | tf_op jit(solution)/shard_map/all_gather | solution.py:18
  216.1 12.1 %copy-start.7 = (f32[1,64,8]{1,2,0:T(8,128)S(1)}, f32[1,64,8]{1,2,0:T(8,128)}, u32[]{:S(2)}) copy-start(f32[1,64,8]{1,2,0:T(8,128)} %param.22) | copy-start | bytes 6148
  216.1 150.0 %all-to-all-start.2 = ((bf16[32,20,2048]{2,1,0:T(8,128)(2,1)}), bf16[32,20,2048]{2,1,0:T(8,128)(2,1)}, u32[]{:S(2)}, u32[]{:S(2)}) async-start(bf16[32,20,2048]{2,1,0:T(8,128)(2,1)} %reshape.208), calls=%async_computation.2 | async-start | bytes 6291456 | tf_op jit(solution)/shard_map/all_to_all | solution.py:101
  373.0 2.4 copy-start.2
Sparse Core Ops, SparseCore 0:
  10.7 105.1 all-gather.2
  119.1 71.6 all-gather.4
where the time goes:
time: 389 us; the launch traced here: 383 us
  waiting for transfers between devices  279 us (72%)
  starting transfers between devices  35.7 us (9%)
  matrix products  23.9 us (6%)
  local copies, waits for them, and re-layouts  19.3 us (5%)
  between operations  13.7 us (4%)
  other arithmetic  11 us (3%)
    all_to_all x1, waiting for transfers between devices, local(): lax.all_to_all(outputs.reshape(sources, items, features), 'expert', split...  138 us
    all_to_all x1, waiting for transfers between devices, local(): lax.all_to_all(outgoing, 'expert', split_axis=0, concat_axis=0, tiled=True)  135 us
    all_to_all x1, starting transfers between devices, local(): lax.all_to_all(outgoing, 'expert', split_axis=0, concat_axis=0, tiled=True)  13.5 us
    all_to_all x1, starting transfers between devices, local(): lax.all_to_all(outputs.reshape(sources, items, features), 'expert', split...  11.8 us
    dot_general x1, matrix products, local(): jnp.dot(slot_rows, server_gate_up[0], preferred_element_type=jnp.float32)  11.1 us
    all_to_all x1, starting transfers between devices, local(): lax.all_to_all(attn_heads, 'dp', split_axis=1, concat_axis=2, tiled=True)  10.2 us
  transfers between devices with their start and end apart: 5, of which 3 were waited for; matrix products, arithmetic and copies ran while one was open for 8% of the time, Pallas kernels for 0%

commit v1 on v0

v1 whole, which is shorter than its diff:
```python
import math

import jax
import jax.numpy as jnp
from jax import lax
from jax.experimental import pallas as pl
from jax.experimental.pallas import tpu as pltpu
from jax.sharding import PartitionSpec as P

MESH = pl.DeviceIdType.MESH
HDIM = 128
TOPK = 8
D = 2048
FF = 1024
NZ = 16
TOK = 64
SUB = TOK // 2
CAP = 20
GRP = 4
GSLOT = GRP * CAP
GTOK = GRP * TOK
NGRP = NZ // GRP
COL = 1024
PAGE = 128
PAGES = COL // PAGE
REQS = 4
QROWS = 256
epsilon = 1e-05

ORDER = (8, 7, 9, 6, 10, 5, 11, 4, 12, 3, 13, 2, 14, 1, 15, 0)
POS = {s: i for i, s in enumerate(ORDER)}

ROWS = (128, 64)
KS = (0, 1, -1, 2)
NMSG = 4 + 4 * len(KS)


def moe_kernel(
    hidden_ref,
    attn_ref,
    gain_ref,
    ids_ref,
    gates_ref,
    gu_hbm,
    dn_hbm,
    out_ref,
    x_buf,
    wg,
    wd,
    gu32,
    dn32,
    xs,
    act,
    outw,
    wcol,
    st,
    ctr,
    rsr,
    rsl,
    resid_s,
    load_sem,
    wsend,
    wrecv,
    sibsend,
    sibrecv,
    agsend,
    agrecv,
    rssend,
    rsrecv,
):
    dp = lax.axis_index("dp")
    ex = lax.axis_index("expert")
    x = dp // 4
    y = ((dp // 2) % 2) * 2 + ex // NZ
    core = dp % 2
    z = ex % NZ

    def dev(xx, yy, zz, cc):
        return ((xx * 2 + yy // 2) * 2 + cc, (yy % 2) * NZ + zz)

    def ring4(v, k):
        return (v + 4 + k) % 4

    sibling = dev(x, y, z, 1 - core)
    zr = dev(x, y, (z + 1) % NZ, core)
    zl = dev(x, y, (z + NZ - 1) % NZ, core)
    xy = {
        (0, 1): dev(ring4(x, 1), y, z, core),
        (0, -1): dev(ring4(x, -1), y, z, core),
        (1, 1): dev(x, ring4(y, 1), z, core),
        (1, -1): dev(x, ring4(y, -1), z, core),
    }

    load_gu = pltpu.make_async_copy(gu_hbm, gu32, load_sem.at[0])
    load_dn = pltpu.make_async_copy(dn_hbm, dn32, load_sem.at[1])
    load_gu.start()
    load_dn.start()

    barrier = pltpu.get_barrier_semaphore()
    partners = [sibling, zr, zl] + list(xy.values())
    for partner in partners:
        pl.semaphore_signal(barrier, inc=1, device_id=partner, device_id_type=MESH)

    pending = []

    def send(src, dst, ssem, rsem, to):
        copy = pltpu.make_async_remote_copy(
            src_ref=src,
            dst_ref=dst,
            send_sem=ssem,
            recv_sem=rsem,
            device_id=to,
            device_id_type=MESH,
        )
        copy.start()
        pending.append(copy)
        return copy

    def arrived(ref, ssem, rsem, to):
        pltpu.make_async_remote_copy(
            src_ref=ref,
            dst_ref=ref,
            send_sem=ssem,
            recv_sem=rsem,
            device_id=to,
            device_id_type=MESH,
        ).wait_recv()

    def shard(stream, dx, dy, off, n):
        sx, sy = ring4(x, -dx), ring4(y, -dy)
        rows = ROWS[stream]
        first = pl.multiple_of(((sx * 2 + sy // 2) * 2 + core) * rows + off, 16)
        buf = wd if stream else wg
        return buf.at[sy % 2, pl.ds(first, n), :]

    def piece(stream, half, k1, k2, part):
        h = ROWS[stream] // 2
        q = h // 2
        off, n = (half * h, h) if part is None else (half * h + part * q, q)
        dx, dy = (k1, k2) if half == 0 else (k2, k1)
        return shard(stream, dx, dy, off, n)

    def wmsg(stream, half, index):
        at = (stream * 2 + half) * NMSG + index
        return wsend.at[at], wrecv.at[at]

    def decode(index):
        if index < 4:
            return 0, (1, -1)[index % 2], index >= 2, 0
        return 1, (1, -1)[index % 2], (index - 4) % 4 >= 2, KS[(index - 4) // 4]

    def wstart(stream, index):
        ring, sign, forward, k = decode(index)
        for half in (0, 1):
            axis = ring if half == 0 else 1 - ring
            part = (0 if sign == 1 else 1) if forward else None
            step = sign if forward else 0
            k1, k2 = (step, 0) if ring == 0 else (k, step)
            ref = piece(stream, half, k1, k2, part)
            ssem, rsem = wmsg(stream, half, index)
            send(ref, ref, ssem, rsem, xy[axis, sign])

    def wwait(stream, index):
        ring, sign, forward, k = decode(index)
        for half in (0, 1):
            axis = ring if half == 0 else 1 - ring
            part = (0 if sign == 1 else 1) if forward else None
            step = 2 if forward else sign
            k1, k2 = (step, 0) if ring == 0 else (k, step)
            ref = piece(stream, half, k1, k2, part)
            ssem, rsem = wmsg(stream, half, index)
            arrived(ref, ssem, rsem, xy[axis, sign])

    def p2(k, j):
        return 4 + 4 * KS.index(k) + j

    sib_index = {}

    def sib(stream, places):
        for dx, dy in places:
            at = stream * 16 + (dx % 4) * 4 + (dy % 4)
            ref = shard(stream, dx, dy, 0, ROWS[stream])
            send(ref, ref, sibsend.at[at], sibrecv.at[at], sibling)
            sib_index[at] = (stream, dx, dy)

    def sib_wait(stream):
        for at, (s, dx, dy) in sib_index.items():
            if s == stream:
                sx, sy = ring4(x, -dx), ring4(y, -dy)
                rows = ROWS[stream]
                first = pl.multiple_of(((sx * 2 + sy // 2) * 2 + 1 - core) * rows, 16)
                buf = wd if stream else wg
                ref = buf.at[sy % 2, pl.ds(first, rows), :]
                arrived(ref, sibsend.at[at], sibrecv.at[at], sibling)

    def weights(stream, phase):
        if phase == 0:
            (load_gu, load_dn)[stream].wait()
            src = (gu32, dn32)[stream]
            rows = ROWS[stream]
            first = pl.multiple_of(dp * rows, 16)
            (wg, wd)[stream][y % 2, pl.ds(first, rows), :] = src[...].astype(jnp.bfloat16)
            if stream == 0:
                pl.semaphore_wait(barrier, len(partners))
            for index in (0, 1, p2(0, 0), p2(0, 1)):
                wstart(stream, index)
            sib(stream, [(0, 0)])
        elif phase == 1:
            for index in (0, 1):
                wwait(stream, index)
            for index in (2, 3, p2(1, 0), p2(1, 1), p2(-1, 0), p2(-1, 1)):
                wstart(stream, index)
        elif phase == 2:
            for index in (p2(0, 0), p2(0, 1)):
                wwait(stream, index)
            for index in (p2(0, 2), p2(0, 3)):
                wstart(stream, index)
            sib(stream, [(1, 0), (-1, 0), (0, 1), (0, -1)])
        elif phase == 3:
            for index in (2, 3):
                wwait(stream, index)
            for index in (p2(2, 0), p2(2, 1)):
                wstart(stream, index)
        elif phase == 4:
            for index in (p2(1, 0), p2(1, 1), p2(-1, 0), p2(-1, 1)):
                wwait(stream, index)
            for index in (p2(1, 2), p2(1, 3), p2(-1, 2), p2(-1, 3)):
                wstart(stream, index)
            sib(stream, [(1, 1), (-1, 1), (1, -1), (-1, -1)])
        elif phase == 5:
            for index in (p2(0, 2), p2(0, 3)):
                wwait(stream, index)
            sib(stream, [(2, 0), (0, 2)])
        elif phase == 6:
            for index in (p2(2, 0), p2(2, 1)):
                wwait(stream, index)
            for index in (p2(2, 2), p2(2, 3)):
                wstart(stream, index)
        elif phase == 7:
            for index in (p2(1, 2), p2(1, 3), p2(-1, 2), p2(-1, 3)):
                wwait(stream, index)
            sib(stream, [(2, 1), (2, -1), (1, 2), (-1, 2)])
        elif phase == 8:
            for index in (p2(2, 2), p2(2, 3)):
                wwait(stream, index)
            sib(stream, [(2, 2)])
            sib_wait(stream)

    def block(source, h):
        return x_buf.at[pl.ds(POS[source] * TOK + h * SUB, SUB), :]

    ag_pending = []

    def ag_start(d, h):
        for way in (0, 1):
            if d == 7 and h != way:
                continue
            src = block((d if way == 0 else NZ - d) % NZ, h)
            dst = block(d + 1 if way == 0 else NZ - d - 1, h)
            at = (way * 8 + d) * 2 + h
            ag_pending.append(
                send(src, dst, agsend.at[at], agrecv.at[at], zr if way == 0 else zl)
            )
            pending.pop()

    def ag_wait(d, h):
        for way in (0, 1):
            if d == 7 and h != way:
                continue
            dst = block(d + 1 if way == 0 else NZ - d - 1, h)
            at = (way * 8 + d) * 2 + h
            arrived(dst, agsend.at[at], agrecv.at[at], zr if way == 0 else zl)

    def ag(i):
        d, h = i // 2, i % 2
        ag_wait(d, h)
        if d < 7:
            ag_start(d + 1, h)

    tri_r = lax.broadcasted_iota(jnp.int32, (GTOK, GTOK), 0)
    tri_c = lax.broadcasted_iota(jnp.int32, (GTOK, GTOK), 1)
    lane = lax.broadcasted_iota(jnp.int32, (8, GTOK), 1)

    def dispatch(g):
        tri = ((tri_r < tri_c) & (tri_r // TOK == tri_c // TOK)).astype(jnp.bfloat16)
        ids = ids_ref[g]
        gates = gates_ref[g]
        marks, shares = [], []
        for e in (0, 1):
            hit = ids == e * NZ + z
            marks.append(jnp.sum(hit.astype(jnp.float32), axis=0, keepdims=True))
            shares.append(jnp.sum(jnp.where(hit, gates, 0.0), axis=0, keepdims=True))
        slot_iota = lax.broadcasted_iota(jnp.int32, (GSLOT, GTOK), 0)
        picks = []
        for e in (0, 1):
            mark = jnp.broadcast_to(marks[e], (8, GTOK))
            earlier = jnp.dot(
                mark.astype(jnp.bfloat16), tri, preferred_element_type=jnp.float32
            )
            slot = jnp.where(
                mark > 0.5, earlier.astype(jnp.int32) + (lane // TOK) * CAP, -1
            )[:1]
            pick = jnp.where(slot_iota == slot, 1.0, 0.0)
            picks.append(pick)
            share = jnp.sum(pick * shares[e], axis=1, keepdims=True)
            wcol[g, pl.ds(e * GSLOT, GSLOT), :] = jnp.broadcast_to(share, (GSLOT, 128))
        pick = jnp.concatenate(picks, axis=0)
        st[g] = pick.T.astype(jnp.bfloat16)
        pick = pick.astype(jnp.bfloat16)
        b, gi = g // 2, g % 2
        for c in range(0, D, 512):
            rows = jnp.dot(
                pick,
                x_buf[pl.ds(g * GTOK, GTOK), pl.ds(c, 512)],
                preferred_element_type=jnp.float32,
            ).astype(jnp.bfloat16)
            for e in (0, 1):
                xs[b, e, pl.ds(gi * GSLOT, GSLOT), pl.ds(c, 512)] = rows[
                    e * GSLOT : (e + 1) * GSLOT
                ]

    def gate_up(b, e):
        def tile(j, carry):
            c0 = pl.multiple_of(j * 256, 256)
            c1 = pl.multiple_of(FF + j * 256, 256)
            lhs = xs[b, e]
            gate = jnp.dot(lhs, wg[e, :, pl.ds(c0, 256)], preferred_element_type=jnp.float32)
            up = jnp.dot(lhs, wg[e, :, pl.ds(c1, 256)], preferred_element_type=jnp.float32)
            hid = gate / (1.0 + jnp.exp(-gate)) * up
            act[b, e, :, pl.ds(c0, 256)] = hid.astype(jnp.bfloat16)
            return carry

        lax.fori_loop(0, FF // 256, tile, 0)

    def down(b, e):
        def tile(j, carry):
            c0 = pl.multiple_of(j * 256, 256)
            res = jnp.dot(
                act[b, e], wd[e, :, pl.ds(c0, 256)], preferred_element_type=jnp.float32
            )
            for gi in (0, 1):
                g = b * 2 + gi
                share = wcol[g, pl.ds(e * GSLOT, GSLOT), :]
                outw[g, pl.ds(e * GSLOT, GSLOT), pl.ds(c0, 256)] = (
                    res[gi * GSLOT : (gi + 1) * GSLOT]
                    * jnp.concatenate([share, share], axis=1)
                ).astype(jnp.bfloat16)
            return carry

        lax.fori_loop(0, D // 256, tile, 0)

    def spread(g):
        def tile(j, carry):
            c0 = pl.multiple_of(j * 256, 256)
            ctr[pl.ds(g * GTOK, GTOK), pl.ds(c0, 256)] = jnp.dot(
                st[g], outw[g, :, pl.ds(c0, 256)], preferred_element_type=jnp.float32
            )
            return carry

        lax.fori_loop(0, D // 256, tile, 0)

    def mine(source, h):
        return ctr[pl.ds(POS[source] * TOK + h * SUB, SUB), :]

    def rs_wait(s, way, h):
        buf = (rsr, rsl)[way].at[s - 1, pl.ds(h * SUB, SUB), :]
        at = (way * 8 + s - 1) * 2 + h
        arrived(buf, rssend.at[at], rsrecv.at[at], zr if way == 0 else zl)
        return buf

    def rs(s):
        for h in (0, 1):
            for way in (0, 1):
                if s == 0 and h != way:
                    continue
                source = 8 + s if way == 0 else 8 - s
                total = mine(source, h)
                if s > 1 or (s == 1 and h == way):
                    total = total + rs_wait(s, way, h)[...].astype(jnp.float32)
                blk = block(source, h)
                blk[...] = total.astype(jnp.bfloat16)
                at = (way * 8 + s) * 2 + h
                dst = (rsr, rsl)[way].at[s, pl.ds(h * SUB, SUB), :]
                send(blk, dst, rssend.at[at], rsrecv.at[at], zr if way == 0 else zl)

    resid = (hidden_ref[...].astype(jnp.float32) + attn_ref[...].astype(jnp.float32)).astype(
        jnp.bfloat16
    )
    resid_s[...] = resid
    resid32 = resid.astype(jnp.float32)
    mean_square = jnp.mean(resid32 * resid32, axis=-1, keepdims=True)
    x_buf[pl.ds(POS[0] * TOK, TOK), :] = (
        resid32 * lax.rsqrt(mean_square + epsilon) * gain_ref[...]
    ).astype(jnp.bfloat16)

    weights(0, 0)
    ag_start(0, 0)
    ag_start(0, 1)
    plan = [
        ("ag", 0), ("ag", 1), ("w", 0, 1), ("ag", 2), ("ag", 3), ("w", 0, 2), ("ag", 4),
        ("ag", 5), ("w", 0, 3), ("dispatch", 3), ("ag", 6), ("ag", 7), ("ag", 8), ("w", 0, 4), ("w", 1, 0),
        ("ag", 9), ("dispatch", 2), ("w", 0, 5), ("ag", 10), ("ag", 11), ("w", 0, 6), ("ag", 12), ("dispatch", 1), ("w", 0, 7),
        ("ag", 13), ("w", 1, 1), ("w", 0, 8), ("ag", 14), ("ag", 15), ("w", 1, 2), ("gate_up", 1, 0),
        ("w", 1, 3), ("dispatch", 0), ("w", 1, 4), ("gate_up", 1, 1), ("w", 1, 5), ("w", 1, 6),
        ("gate_up", 0, 0), ("w", 1, 7), ("gate_up", 0, 1), ("w", 1, 8), ("agdone",),
        ("down", 0, 0), ("down", 0, 1), ("spread", 0), ("rs", 0), ("rs", 1), ("spread", 1), ("rs", 2),
        ("down", 1, 0), ("rs", 3), ("down", 1, 1), ("spread", 2), ("rs", 4), ("spread", 3),
        ("rs", 5), ("rs", 6), ("rs", 7),
    ]

    def ag_done():
        for copy in ag_pending:
            copy.wait_send()

    run = {
        "ag": ag, "w": weights, "dispatch": dispatch, "gate_up": gate_up, "down": down,
        "spread": spread, "rs": rs, "agdone": ag_done,
    }
    for name, *args in plan:
        run[name](*args)

    for h in (0, 1):
        total = resid_s[pl.ds(h * SUB, SUB), :].astype(jnp.float32) + mine(0, h)
        for way in (0, 1):
            total = total + rs_wait(8, way, h)[...].astype(jnp.float32)
        out_ref[pl.ds(h * SUB, SUB), :] = total.astype(jnp.bfloat16)
    for copy in pending:
        copy.wait_send()


def moe(hidden, attn, gain, ids, gates, gate_up, down):
    vmem = pl.BlockSpec(memory_space=pltpu.VMEM)
    hbm = pl.BlockSpec(memory_space=pl.ANY)
    bf, f32 = jnp.bfloat16, jnp.float32
    dma = pltpu.SemaphoreType.DMA
    return pl.pallas_call(
        moe_kernel,
        out_shape=jax.ShapeDtypeStruct((TOK, D), bf),
        in_specs=[vmem] * 5 + [hbm] * 2,
        out_specs=vmem,
        scratch_shapes=[
            pltpu.VMEM((NZ * TOK, D), bf),
            pltpu.VMEM((2, D, 2 * FF), bf),
            pltpu.VMEM((2, FF, D), bf),
            pltpu.VMEM((ROWS[0], D), f32),
            pltpu.VMEM((ROWS[1], D), f32),
            pltpu.VMEM((2, 2, 2 * GSLOT, D), bf),
            pltpu.VMEM((2, 2, 2 * GSLOT, FF), bf),
            pltpu.VMEM((NGRP, 2 * GSLOT, D), bf),
            pltpu.VMEM((NGRP, 2 * GSLOT, 128), f32),
            pltpu.VMEM((NGRP, GTOK, 2 * GSLOT), bf),
            pltpu.VMEM((NZ * TOK, D), f32),
            pltpu.VMEM((8, TOK, D), bf),
            pltpu.VMEM((8, TOK, D), bf),
            pltpu.VMEM((TOK, D), bf),
            dma((2,)),
            dma((4 * NMSG,)),
            dma((4 * NMSG,)),
            dma((32,)),
            dma((32,)),
            dma((32,)),
            dma((32,)),
            dma((32,)),
            dma((32,)),
        ],
        compiler_params=pltpu.CompilerParams(
            collective_id=0, has_side_effects=True, vmem_limit_bytes=56 * 1024 * 1024
        ),
    )(hidden, attn, gain, ids, gates, gate_up, down)


def attention_kernel(table_ref, length_ref, q_ref, k_ref, v_ref, out_ref, keys, values):
    for p in range(PAGES):
        at = table_ref[0, p]
        keys[pl.ds(p * PAGE, PAGE), :] = k_ref[at]
        values[pl.ds(p * PAGE, PAGE), :] = v_ref[at]
    scale = 1.0 / math.sqrt(HDIM)
    key_at = lax.broadcasted_iota(jnp.int32, (1, COL), 1)
    end = jnp.int32(0)
    ends = []
    for r in range(REQS):
        end = end + length_ref[0, r]
        ends.append(end)
    key_request = sum((key_at >= e).astype(jnp.int32) for e in ends)

    def block(i, carry):
        first = pl.multiple_of(i * QROWS, QROWS)
        row_at = first + lax.broadcasted_iota(jnp.int32, (QROWS, 1), 0)
        row_request = sum((row_at >= e).astype(jnp.int32) for e in ends)
        scores = (
            lax.dot_general(
                q_ref[pl.ds(first, QROWS), :],
                keys[...],
                (((1,), (1,)), ((), ())),
                preferred_element_type=jnp.float32,
            )
            * scale
        )
        scores = jnp.where(row_request == key_request, scores, -1e30)
        highest = jnp.max(scores, axis=-1, keepdims=True)
        weights = jnp.exp(scores - highest)
        totals = jnp.sum(weights, axis=-1, keepdims=True)
        probs = (weights * (1.0 / totals)).astype(jnp.bfloat16)
        out_ref[pl.ds(first, QROWS), :] = jnp.dot(
            probs, values[...], preferred_element_type=jnp.float32
        ).astype(jnp.bfloat16)
        return carry

    lax.fori_loop(0, COL // QROWS, block, 0)


def attention(queries, key_pool, value_pool, page_table, prompt_lengths):
    vmem = pl.BlockSpec(memory_space=pltpu.VMEM)
    smem = pl.BlockSpec(memory_space=pltpu.SMEM)
    return pl.pallas_call(
        attention_kernel,
        out_shape=jax.ShapeDtypeStruct((COL, HDIM), jnp.bfloat16),
        in_specs=[smem, smem, vmem, vmem, vmem],
        out_specs=vmem,
        scratch_shapes=[
            pltpu.VMEM((COL, HDIM), jnp.bfloat16),
            pltpu.VMEM((COL, HDIM), jnp.bfloat16),
        ],
        compiler_params=pltpu.CompilerParams(vmem_limit_bytes=16 * 1024 * 1024),
    )(page_table, prompt_lengths, queries, key_pool, value_pool)


def local(
    hidden_in,
    queries,
    key_pool,
    value_pool,
    page_table,
    prompt_lengths,
    expert_ids,
    gate_weights,
    norm_gain,
    trainer_gate_up,
    trainer_down,
):
    routing = jnp.concatenate([expert_ids[0].astype(jnp.float32), gate_weights[0]], axis=1)
    rings = [[half * NZ + k for k in range(NZ)] for half in range(2)]
    routing = lax.all_gather(routing.T, "expert", axis_index_groups=rings)
    z = lax.axis_index("expert") % NZ
    behind = lax.rev(routing, (0,))
    behind = jnp.concatenate([behind, behind], axis=0)
    behind = lax.dynamic_slice_in_dim(behind, NZ - 1 - z, NZ, axis=0)
    routing = jnp.stack(
        [
            jnp.concatenate([behind[s] for s in ORDER[g * GRP : (g + 1) * GRP]], axis=1)
            for g in range(NGRP)
        ]
    )
    ids, gates = routing[:, :TOPK].astype(jnp.int32), routing[:, TOPK:]

    attn_heads = attention(queries[0], key_pool, value_pool, page_table, prompt_lengths)
    attn_tokens = lax.all_to_all(attn_heads[None], "dp", split_axis=1, concat_axis=2, tiled=True)
    mixed = moe(
        hidden_in[0],
        attn_tokens[0],
        norm_gain[None],
        ids,
        gates,
        trainer_gate_up[0],
        trainer_down[0],
    )
    return mixed[None]


def solution(mesh):
    placed = (
        P("expert", "dp", None),
        P("expert", None, "dp"),
        P("expert", None, "dp"),
        P("expert", None, "dp"),
        P("expert", None),
        P("expert", None),
        P("expert", "dp", None),
        P("expert", "dp", None),
        P(),
        P("expert", "dp", None),
        P("expert", "dp", None),
    )
    return jax.shard_map(
        local, mesh=mesh, in_specs=placed, out_specs=P("expert", "dp", None), check_vma=False
    )
```

time: 389 us -> 189 us (0.49); the launches traced: 383 us -> 188 us
  waiting for transfers between devices: 279 us -> 0.01 us
  Pallas kernels: 0 us -> 137 us
  blocking collectives: 0 us -> 27.6 us
  starting transfers between devices: 35.7 us -> 10.2 us
  matrix products: 23.9 us -> 0 us
  between operations: 13.7 us -> 0.11 us
  local copies, waits for them, and re-layouts: 19.3 us -> 9.51 us
  other arithmetic: 11 us -> 3.07 us
    all_to_all x3 -> x1, waiting for transfers between devices: 279 us -> 0.01 us  [local(): lax.all_to_all(attn_heads[None], 'dp', split_axis=1, concat_axis=2, tiled...]
    pallas_call x0 -> x2, Pallas kernels: none -> 137 us  [the longest x1 133 us: moe(): pl.pallas_call(moe_kernel, out_shape=jax.ShapeDtypeStruct((TOK, D), bf),...]
    all_gather x0 -> x1, blocking collectives: none -> 27.6 us  [local(): routing = lax.all_gather(routing.T, 'expert', axis_index_groups=rings)]
    all_to_all x3 -> x1, starting transfers between devices: 35.5 us -> 10.2 us  [local(): lax.all_to_all(attn_heads[None], 'dp', split_axis=1, concat_axis=2, tiled...]
    dot_general x8 -> x0, matrix products: 23.9 us -> none  [the longest x1 11.1 us: local(): jnp.dot(slot_rows, server_gate_up[0], preferred_element_type=jnp.float32)]
    reshape x6 -> x0, local copies, waits for them, and re-layouts: 11 us -> none  [the longest x1 3.64 us: local(): returned.reshape(expert_count * capacity, width)]
    unnamed x26 -> x20, local copies, waits for them, and re-layouts: 2.36 us -> 8.9 us
    gather x3 -> x0, local copies, waits for them, and re-layouts: 4.54 us -> none  [the longest x1 3.35 us: local(): jnp.take(returned.reshape(expert_count * capacity, width), flat_slot, axi...]
  transfers between devices with their start and end apart: 5 -> 1, of which waited for: 3 -> 0; matrix products, arithmetic and copies ran while one was open for 8% -> 0% of each run, Pallas kernels for 0% -> 0%
where the time goes in v1:
time: 189 us; the launch traced here: 188 us
  Pallas kernels  137 us (72%)
  blocking collectives  27.6 us (15%)
  starting transfers between devices  10.2 us (5%)
  local copies, waits for them, and re-layouts  9.51 us (5%)
  other arithmetic  3.07 us (2%)
    pallas_call x1, Pallas kernels, moe(): pl.pallas_call(moe_kernel, out_shape=jax.ShapeDtypeStruct((TOK, D), bf),...  133 us
    all_gather x1, blocking collectives, local(): routing = lax.all_gather(routing.T, 'expert', axis_index_groups=rings)  27.6 us
    all_to_all x1, starting transfers between devices, local(): lax.all_to_all(attn_heads[None], 'dp', split_axis=1, concat_axis=2, tiled...  10.2 us
    unnamed x20, local copies, waits for them, and re-layouts  8.9 us
  transfers between devices with their start and end apart: 1, of which 0 were waited for; matrix products, arithmetic and copies ran while one was open for 0% of the time, Pallas kernels for 0%

profile of v1, /device:TPU:1, one launch (start us, length us, event | category | flops | bytes accessed | tf_op | source)
XLA Modules:
  0.0 187.7 jit_solution(1695754043451127599)
XLA Ops:
  0.0 0.0 copy-start.3
  0.0 0.7 copy-done.3
  0.7 0.0 copy-done.4
  0.7 0.9 copy-done
  1.6 0.9 copy-done.1
  2.6 0.9 copy-done.2
  3.5 3.8 %shard_map.109 = bf16[1024,128]{1,0:T(8,128)(2,1)S(1)} custom-call(s32[1,8]{1,0:T(1,128)S(1)} %copy-done.3, s32[1,4]{1,0:T(1,128)S(1)} %copy-done.4, bf16[1024,128]{1,0:T(8,128)(2,1)S(1)} %bitcast.66, bf16[8,128,128]{2,1,0:T(8,128)(2,1)S(1)} %copy-done.1, bf16[8,128,128]{2,1,0:T(8,128)(2,1)S(1)} %copy-done.2), custom_call_target="tpu_custom_call" | custom-call | tf_op jit(solution)/shard_map/pallas_call | solution.py:515
  7.3 0.4 copy.22
  7.7 0.5 broadcast.1
  8.2 2.2 %reduce = bf16[1024,128]{1,0:T(8,128)(2,1)S(1)} reduce(bf16[1024,1,128]{2,1,0:T(2,128)(2,1)S(1)} %bitcast.68, bf16[]{:T(256)} %broadcast.1), dimensions={1}, to_apply=%bitcast.64.reduce_sub_computation | reduce | bytes 524290
  10.4 0.8 reshape.3
  11.2 10.2 %all-to-all-start = ((bf16[16,2,4096]{2,1,0:T(2,128)(2,1)}), bf16[16,2,4096]{2,1,0:T(2,128)(2,1)S(1)}, u32[]{:S(2)}, u32[]{:S(2)}) async-start(bf16[16,2,4096]{2,1,0:T(2,128)(2,1)} %reshape.3), calls=%async_computation | async-start | bytes 524288 | tf_op jit(solution)/shard_map/all_to_all | solution.py:557
  21.4 0.7 copy-done.5
  22.1 0.7 copy-done.6
  22.8 27.6 %all-gather = f32[256,64]{1,0:T(8,128)S(1)} all-gather(f32[16,64]{1,0:T(8,128)S(1)} %maximum_bitcast_fusion.4), channel_id=2, replica_groups={{0,1,2,3,4,5,6,7,8,9,10,11,12,13,14,15},{16,17,18,19,20,21,22,23,24,25,..., dimensions={0}, use_global_device_ids=true | all-gather | bytes 69632 | tf_op jit(solution)/shard_map/all_gather | solution.py:543
  50.5 0.1 maximum_bitcast_fusion.2
  50.5 0.1 maximum_bitcast_fusion
  50.6 0.6 fusion.1
  51.3 0.0 all-to-all-done
  51.3 0.3 reshape.4
  51.6 0.2 copy.16
  51.8 0.8 copy.21
  52.6 133.5 %shard_map.110 = bf16[64,2048]{1,0:T(8,128)(2,1)} custom-call(bf16[64,2048]{1,0:T(8,128)(2,1)} %bitcast.76, bf16[64,2048]{1,0:T(8,128)(2,1)} %bitcast.70, f32[1,2048]{1,0:T(1,128)} %bitcast.77, s32[4,8,256]{2,1,0:T(8,128)} %get-tuple-element.22.ids_ref, f32[4,8,256]{2,1,0:T(8,128)} %get-tuple-element.21.gates_ref, f32[128,2048]{1,0:T(8,128)} %bitcast.69, ...), custom_call_target="tpu_custom_call" | custom-call | tf_op jit(solution)/shard_map/pallas_call | solution.py:436
  186.0 1.7 copy.24
  (13 shorter events, 0.1 us)
Async XLA Ops:
  0.0 0.7 copy-start.3
  0.0 0.7 copy-start.4
  0.7 0.9 copy-start
  1.6 0.9 copy-start.1
  2.6 0.9 copy-start.2
  11.2 40.1 %all-to-all-start = ((bf16[16,2,4096]{2,1,0:T(2,128)(2,1)}), bf16[16,2,4096]{2,1,0:T(2,128)(2,1)S(1)}, u32[]{:S(2)}, u32[]{:S(2)}) async-start(bf16[16,2,4096]{2,1,0:T(2,128)(2,1)} %reshape.3), calls=%async_computation | async-start | bytes 524288 | tf_op jit(solution)/shard_map/all_to_all | solution.py:557
  21.4 0.7 copy-start.5
  22.1 0.7 copy-start.6

commit v2 on v1

--- a/solution.py
+++ b/solution.py
@@ -13,6 +13,7 @@
 D = 2048
 FF = 1024
 NZ = 16
+NDP = 16
 TOK = 64
 SUB = TOK // 2
 CAP = 20
@@ -36,14 +37,22 @@
 
 
 def moe_kernel(
+    table_ref,
+    length_ref,
+    q_ref,
+    k_ref,
+    v_ref,
     hidden_ref,
-    attn_ref,
     gain_ref,
-    ids_ref,
-    gates_ref,
+    routing_ref,
     gu_hbm,
     dn_hbm,
     out_ref,
+    keys,
+    values,
+    heads_out,
+    heads_in,
+    route,
     x_buf,
     wg,
     wd,
@@ -67,6 +76,10 @@
     agrecv,
     rssend,
     rsrecv,
+    hsend,
+    hrecv,
+    rtsend,
+    rtrecv,
 ):
     dp = lax.axis_index("dp")
     ex = lax.axis_index("expert")
@@ -97,7 +110,8 @@
     load_dn.start()
 
     barrier = pltpu.get_barrier_semaphore()
-    partners = [sibling, zr, zl] + list(xy.values())
+    peers = [((dp + k) % NDP, ex) for k in range(1, NDP)]
+    partners = peers + [zr, zl, xy[1, 1], xy[1, -1]]
     for partner in partners:
         pl.semaphore_signal(barrier, inc=1, device_id=partner, device_id_type=MESH)
 
@@ -262,6 +276,15 @@
                 send(src, dst, agsend.at[at], agrecv.at[at], zr if way == 0 else zl)
             )
             pending.pop()
+            if h == 0 and not (d == 7 and way == 1):
+                at = way * 8 + d
+                send(
+                    route.at[(d if way == 0 else NZ - d) % NZ],
+                    route.at[d + 1 if way == 0 else NZ - d - 1],
+                    rtsend.at[at],
+                    rtrecv.at[at],
+                    zr if way == 0 else zl,
+                )
 
     def ag_wait(d, h):
         for way in (0, 1):
@@ -270,6 +293,14 @@
             dst = block(d + 1 if way == 0 else NZ - d - 1, h)
             at = (way * 8 + d) * 2 + h
             arrived(dst, agsend.at[at], agrecv.at[at], zr if way == 0 else zl)
+            if h == 0 and not (d == 7 and way == 1):
+                at = way * 8 + d
+                arrived(
+                    route.at[d + 1 if way == 0 else NZ - d - 1],
+                    rtsend.at[at],
+                    rtrecv.at[at],
+                    zr if way == 0 else zl,
+                )
 
     def ag(i):
         d, h = i // 2, i % 2
@@ -283,11 +314,12 @@
 
     def dispatch(g):
         tri = ((tri_r < tri_c) & (tri_r // TOK == tri_c // TOK)).astype(jnp.bfloat16)
-        ids = ids_ref[g]
-        gates = gates_ref[g]
+        parts = [route[s] for s in ORDER[g * GRP : (g + 1) * GRP]]
+        parts = jnp.concatenate([part[:, :TOK] for part in parts], axis=1)
+        ids, gates = parts[:TOPK], parts[TOPK:]
         marks, shares = [], []
         for e in (0, 1):
-            hit = ids == e * NZ + z
+            hit = ids == (e * NZ + z).astype(jnp.float32)
             marks.append(jnp.sum(hit.astype(jnp.float32), axis=0, keepdims=True))
             shares.append(jnp.sum(jnp.where(hit, gates, 0.0), axis=0, keepdims=True))
         slot_iota = lax.broadcasted_iota(jnp.int32, (GSLOT, GTOK), 0)
@@ -383,21 +415,75 @@
                 dst = (rsr, rsl)[way].at[s, pl.ds(h * SUB, SUB), :]
                 send(blk, dst, rssend.at[at], rsrecv.at[at], zr if way == 0 else zl)
 
-    resid = (hidden_ref[...].astype(jnp.float32) + attn_ref[...].astype(jnp.float32)).astype(
-        jnp.bfloat16
-    )
-    resid_s[...] = resid
-    resid32 = resid.astype(jnp.float32)
-    mean_square = jnp.mean(resid32 * resid32, axis=-1, keepdims=True)
+    route[0] = routing_ref[...]
+    weights(0, 0)
+
+    for p in range(PAGES):
+        at = table_ref[0, p]
+        keys[pl.ds(p * PAGE, PAGE), :] = k_ref[at]
+        values[pl.ds(p * PAGE, PAGE), :] = v_ref[at]
+    scale = 1.0 / math.sqrt(HDIM)
+    key_at = lax.broadcasted_iota(jnp.int32, (1, COL), 1)
+    end = jnp.int32(0)
+    ends = []
+    for r in range(REQS):
+        end = end + length_ref[0, r]
+        ends.append(end)
+    key_request = sum((key_at >= e).astype(jnp.int32) for e in ends)
+
+    def attend(i, carry):
+        first = pl.multiple_of(i * QROWS, QROWS)
+        row_at = first + lax.broadcasted_iota(jnp.int32, (QROWS, 1), 0)
+        row_request = sum((row_at >= e).astype(jnp.int32) for e in ends)
+        scores = (
+            lax.dot_general(
+                q_ref[pl.ds(first, QROWS), :],
+                keys[...],
+                (((1,), (1,)), ((), ())),
+                preferred_element_type=jnp.float32,
+            )
+            * scale
+        )
+        scores = jnp.where(row_request == key_request, scores, -1e30)
+        highest = jnp.max(scores, axis=-1, keepdims=True)
+        share = jnp.exp(scores - highest)
+        totals = jnp.sum(share, axis=-1, keepdims=True)
+        probs = (share * (1.0 / totals)).astype(jnp.bfloat16)
+        heads_out[pl.ds(first, QROWS), :] = jnp.dot(
+            probs, values[...], preferred_element_type=jnp.float32
+        ).astype(jnp.bfloat16)
+        return carry
+
+    lax.fori_loop(0, COL // QROWS, attend, 0)
+    for k in range(1, NDP):
+        to = (dp + k) % NDP
+        send(
+            heads_out.at[pl.ds(pl.multiple_of(to * TOK, TOK), TOK), :],
+            heads_in.at[k],
+            hsend.at[k],
+            hrecv.at[k],
+            peers[k - 1],
+        )
+    heads_in[0] = heads_out[pl.ds(pl.multiple_of(dp * TOK, TOK), TOK), :]
+    weights(0, 1)
+    for k in range(1, NDP):
+        arrived(heads_in.at[k], hsend.at[k], hrecv.at[k], peers[k - 1])
+    squares = jnp.zeros((TOK, HDIM), jnp.float32)
+    for h in range(NDP):
+        cols = pl.ds(h * HDIM, HDIM)
+        attn = heads_in[(dp + NDP - h) % NDP].astype(jnp.float32)
+        resid = (hidden_ref[:, cols].astype(jnp.float32) + attn).astype(jnp.bfloat16)
+        resid_s[:, cols] = resid
+        squares = squares + resid.astype(jnp.float32) * resid.astype(jnp.float32)
+    factor = lax.rsqrt(jnp.sum(squares, axis=-1, keepdims=True) * (1.0 / D) + epsilon)
     x_buf[pl.ds(POS[0] * TOK, TOK), :] = (
-        resid32 * lax.rsqrt(mean_square + epsilon) * gain_ref[...]
+        resid_s[...].astype(jnp.float32) * factor * gain_ref[...]
     ).astype(jnp.bfloat16)
 
-    weights(0, 0)
     ag_start(0, 0)
     ag_start(0, 1)
     plan = [
-        ("ag", 0), ("ag", 1), ("w", 0, 1), ("ag", 2), ("ag", 3), ("w", 0, 2), ("ag", 4),
+        ("ag", 0), ("ag", 1), ("ag", 2), ("ag", 3), ("w", 0, 2), ("ag", 4),
         ("ag", 5), ("w", 0, 3), ("dispatch", 3), ("ag", 6), ("ag", 7), ("ag", 8), ("w", 0, 4), ("w", 1, 0),
         ("ag", 9), ("dispatch", 2), ("w", 0, 5), ("ag", 10), ("ag", 11), ("w", 0, 6), ("ag", 12), ("dispatch", 1), ("w", 0, 7),
         ("ag", 13), ("w", 1, 1), ("w", 0, 8), ("ag", 14), ("ag", 15), ("w", 1, 2), ("gate_up", 1, 0),
@@ -428,17 +514,23 @@
         copy.wait_send()
 
 
-def moe(hidden, attn, gain, ids, gates, gate_up, down):
+def moe(table, lengths, queries, keys, values, hidden, gain, routing, gate_up, down):
     vmem = pl.BlockSpec(memory_space=pltpu.VMEM)
+    smem = pl.BlockSpec(memory_space=pltpu.SMEM)
     hbm = pl.BlockSpec(memory_space=pl.ANY)
     bf, f32 = jnp.bfloat16, jnp.float32
     dma = pltpu.SemaphoreType.DMA
     return pl.pallas_call(
         moe_kernel,
         out_shape=jax.ShapeDtypeStruct((TOK, D), bf),
-        in_specs=[vmem] * 5 + [hbm] * 2,
+        in_specs=[smem] * 2 + [vmem] * 6 + [hbm] * 2,
         out_specs=vmem,
         scratch_shapes=[
+            pltpu.VMEM((COL, HDIM), bf),
+            pltpu.VMEM((COL, HDIM), bf),
+            pltpu.VMEM((COL, HDIM), bf),
+            pltpu.VMEM((NDP, TOK, HDIM), bf),
+            pltpu.VMEM((NZ, 2 * TOPK, 2 * TOK), f32),
             pltpu.VMEM((NZ * TOK, D), bf),
             pltpu.VMEM((2, D, 2 * FF), bf),
             pltpu.VMEM((2, FF, D), bf),
@@ -462,67 +554,15 @@
             dma((32,)),
             dma((32,)),
             dma((32,)),
+            dma((NDP,)),
+            dma((NDP,)),
+            dma((16,)),
+            dma((16,)),
         ],
         compiler_params=pltpu.CompilerParams(
             collective_id=0, has_side_effects=True, vmem_limit_bytes=56 * 1024 * 1024
         ),
-    )(hidden, attn, gain, ids, gates, gate_up, down)
-
-
-def attention_kernel(table_ref, length_ref, q_ref, k_ref, v_ref, out_ref, keys, values):
-    for p in range(PAGES):
-        at = table_ref[0, p]
-        keys[pl.ds(p * PAGE, PAGE), :] = k_ref[at]
-        values[pl.ds(p * PAGE, PAGE), :] = v_ref[at]
-    scale = 1.0 / math.sqrt(HDIM)
-    key_at = lax.broadcasted_iota(jnp.int32, (1, COL), 1)
-    end = jnp.int32(0)
-    ends = []
-    for r in range(REQS):
-        end = end + length_ref[0, r]
-        ends.append(end)
-    key_request = sum((key_at >= e).astype(jnp.int32) for e in ends)
-
-    def block(i, carry):
-        first = pl.multiple_of(i * QROWS, QROWS)
-        row_at = first + lax.broadcasted_iota(jnp.int32, (QROWS, 1), 0)
-        row_request = sum((row_at >= e).astype(jnp.int32) for e in ends)
-        scores = (
-            lax.dot_general(
-                q_ref[pl.ds(first, QROWS), :],
-                keys[...],
-                (((1,), (1,)), ((), ())),
-                preferred_element_type=jnp.float32,
-            )
-            * scale
-        )
-        scores = jnp.where(row_request == key_request, scores, -1e30)
-        highest = jnp.max(scores, axis=-1, keepdims=True)
-        weights = jnp.exp(scores - highest)
-        totals = jnp.sum(weights, axis=-1, keepdims=True)
-        probs = (weights * (1.0 / totals)).astype(jnp.bfloat16)
-        out_ref[pl.ds(first, QROWS), :] = jnp.dot(
-            probs, values[...], preferred_element_type=jnp.float32
-        ).astype(jnp.bfloat16)
-        return carry
-
-    lax.fori_loop(0, COL // QROWS, block, 0)
-
-
-def attention(queries, key_pool, value_pool, page_table, prompt_lengths):
-    vmem = pl.BlockSpec(memory_space=pltpu.VMEM)
-    smem = pl.BlockSpec(memory_space=pltpu.SMEM)
-    return pl.pallas_call(
-        attention_kernel,
-        out_shape=jax.ShapeDtypeStruct((COL, HDIM), jnp.bfloat16),
-        in_specs=[smem, smem, vmem, vmem, vmem],
-        out_specs=vmem,
-        scratch_shapes=[
-            pltpu.VMEM((COL, HDIM), jnp.bfloat16),
-            pltpu.VMEM((COL, HDIM), jnp.bfloat16),
-        ],
-        compiler_params=pltpu.CompilerParams(vmem_limit_bytes=16 * 1024 * 1024),
-    )(page_table, prompt_lengths, queries, key_pool, value_pool)
+    )(table, lengths, queries, keys, values, hidden, gain, routing, gate_up, down)
 
 
 def local(
@@ -539,28 +579,16 @@
     trainer_down,
 ):
     routing = jnp.concatenate([expert_ids[0].astype(jnp.float32), gate_weights[0]], axis=1)
-    rings = [[half * NZ + k for k in range(NZ)] for half in range(2)]
-    routing = lax.all_gather(routing.T, "expert", axis_index_groups=rings)
-    z = lax.axis_index("expert") % NZ
-    behind = lax.rev(routing, (0,))
-    behind = jnp.concatenate([behind, behind], axis=0)
-    behind = lax.dynamic_slice_in_dim(behind, NZ - 1 - z, NZ, axis=0)
-    routing = jnp.stack(
-        [
-            jnp.concatenate([behind[s] for s in ORDER[g * GRP : (g + 1) * GRP]], axis=1)
-            for g in range(NGRP)
-        ]
-    )
-    ids, gates = routing[:, :TOPK].astype(jnp.int32), routing[:, TOPK:]
-
-    attn_heads = attention(queries[0], key_pool, value_pool, page_table, prompt_lengths)
-    attn_tokens = lax.all_to_all(attn_heads[None], "dp", split_axis=1, concat_axis=2, tiled=True)
+    routing = jnp.pad(routing.T, ((0, 0), (0, TOK)))
     mixed = moe(
+        page_table,
+        prompt_lengths,
+        queries[0],
+        key_pool,
+        value_pool,
         hidden_in[0],
-        attn_tokens[0],
         norm_gain[None],
-        ids,
-        gates,
+        routing,
         trainer_gate_up[0],
         trainer_down[0],
     )

time: 189 us -> 158 us (0.84)
  blocking collectives: 27.6 us -> 0 us
  Pallas kernels: 137 us -> 154 us
  starting transfers between devices: 10.2 us -> 0 us
  local copies, waits for them, and re-layouts: 9.51 us -> 3.64 us
  other arithmetic: 3.07 us -> 0.01 us
    all_gather x1 -> x0, blocking collectives: 27.6 us -> none  [local(): routing = lax.all_gather(routing.T, 'expert', axis_index_groups=rings)]
    pallas_call x1, Pallas kernels: 133 us -> 154 us  [moe(): pl.pallas_call(moe_kernel, out_shape=jax.ShapeDtypeStruct((TOK, D), bf),...]
    all_to_all x1 -> x0, starting transfers between devices: 10.2 us -> none  [local(): lax.all_to_all(attn_heads[None], 'dp', split_axis=1, concat_axis=2, tiled...]
    unnamed x20 -> x5, local copies, waits for them, and re-layouts: 8.9 us -> 3.04 us
    pallas_call x1 -> x0, Pallas kernels: 3.77 us -> none  [attention(): pl.pallas_call(attention_kernel, out_shape=jax.ShapeDtypeStruct((COL, HDI...]
    unnamed x1 -> x0, other arithmetic: 2.21 us -> none
  transfers between devices with their start and end apart: 1 -> 0, of which waited for: 0 -> 0; matrix products, arithmetic and copies ran while one was open for 0% -> 0% of each run, Pallas kernels for 0% -> 0%
where the time goes in v2:
time: 158 us
  Pallas kernels  154 us (97%)
  local copies, waits for them, and re-layouts  3.64 us (2%)
    pallas_call x1, Pallas kernels, moe(): pl.pallas_call(moe_kernel, out_shape=jax.ShapeDtypeStruct((TOK, D), bf),...  154 us

profile of v2, /device:TPU:1, one launch (start us, length us, event | category | flops | bytes accessed | tf_op | source)
XLA Modules:
  0.0 158.1 jit_solution(13533600861653411892)
XLA Ops:
  0.0 0.0 copy-start
  0.0 0.7 copy-done
  0.7 0.0 copy-start.1
  0.7 0.7 copy-done.1
  1.4 0.6 pad.4.routing_ref
  2.0 154.5 %shard_map.109 = bf16[64,2048]{1,0:T(8,128)(2,1)} custom-call(s32[1,8]{1,0:T(1,128)} %table_ref.1, s32[1,4]{1,0:T(1,128)} %length_ref.1, bf16[1024,128]{1,0:T(8,128)(2,1)} %bitcast.14, bf16[8,128,128]{2,1,0:T(8,128)(2,1)} %k_ref.1, bf16[8,128,128]{2,1,0:T(8,128)(2,1)} %v_ref.1, bf16[64,2048]{1,0:T(8,128)(2,1)} %bitcast.15, f32[1,2048]{1,0:T(1,128)} %bitcast.16, ...), custom_call_target="tpu_custom_call" | custom-call | tf_op jit(solution)/shard_map/pallas_call | solution.py:523
  156.5 1.7 %copy.13 = bf16[1,64,2048]{2,1,0:T(8,128)(2,1)} copy(bf16[1,64,2048]{2,1,0:T(8,128)(2,1)} %bitcast.12) | data formatting | bytes 524288
  (2 shorter events, 0.0 us)
Async XLA Ops:
  0.0 0.7 copy-start
  0.7 0.7 copy-start.1

commit v3 on v2

--- a/solution.py
+++ b/solution.py
@@ -21,6 +21,8 @@
 GSLOT = GRP * CAP
 GTOK = GRP * TOK
 NGRP = NZ // GRP
+WIDE = 512
+HALF = D // 2
 COL = 1024
 PAGE = 128
 PAGES = COL // PAGE
@@ -351,69 +353,55 @@
                     e * GSLOT : (e + 1) * GSLOT
                 ]
 
-    def gate_up(b, e):
-        def tile(j, carry):
-            c0 = pl.multiple_of(j * 256, 256)
-            c1 = pl.multiple_of(FF + j * 256, 256)
-            lhs = xs[b, e]
-            gate = jnp.dot(lhs, wg[e, :, pl.ds(c0, 256)], preferred_element_type=jnp.float32)
-            up = jnp.dot(lhs, wg[e, :, pl.ds(c1, 256)], preferred_element_type=jnp.float32)
-            hid = gate / (1.0 + jnp.exp(-gate)) * up
-            act[b, e, :, pl.ds(c0, 256)] = hid.astype(jnp.bfloat16)
-            return carry
-
-        lax.fori_loop(0, FF // 256, tile, 0)
-
-    def down(b, e):
-        def tile(j, carry):
-            c0 = pl.multiple_of(j * 256, 256)
-            res = jnp.dot(
-                act[b, e], wd[e, :, pl.ds(c0, 256)], preferred_element_type=jnp.float32
-            )
-            for gi in (0, 1):
-                g = b * 2 + gi
-                share = wcol[g, pl.ds(e * GSLOT, GSLOT), :]
-                outw[g, pl.ds(e * GSLOT, GSLOT), pl.ds(c0, 256)] = (
-                    res[gi * GSLOT : (gi + 1) * GSLOT]
-                    * jnp.concatenate([share, share], axis=1)
-                ).astype(jnp.bfloat16)
-            return carry
-
-        lax.fori_loop(0, D // 256, tile, 0)
-
-    def spread(g):
-        def tile(j, carry):
-            c0 = pl.multiple_of(j * 256, 256)
-            ctr[pl.ds(g * GTOK, GTOK), pl.ds(c0, 256)] = jnp.dot(
-                st[g], outw[g, :, pl.ds(c0, 256)], preferred_element_type=jnp.float32
-            )
-            return carry
-
-        lax.fori_loop(0, D // 256, tile, 0)
-
-    def mine(source, h):
-        return ctr[pl.ds(POS[source] * TOK + h * SUB, SUB), :]
+    def gate_up(b, e, j):
+        lhs = xs[b, e]
+        cols = pl.ds(j * 256, 256)
+        gate = jnp.dot(lhs, wg[e, :, cols], preferred_element_type=jnp.float32)
+        up = jnp.dot(
+            lhs, wg[e, :, pl.ds(FF + j * 256, 256)], preferred_element_type=jnp.float32
+        )
+        hid = gate / (1.0 + jnp.exp(-gate)) * up
+        act[b, e, :, cols] = hid.astype(jnp.bfloat16)
+
+    def down(b, e, j):
+        cols = pl.ds(j * WIDE, WIDE)
+        res = jnp.dot(act[b, e], wd[e, :, cols], preferred_element_type=jnp.float32)
+        for gi in (0, 1):
+            g = b * 2 + gi
+            share = wcol[g, pl.ds(e * GSLOT, GSLOT), :]
+            share = jnp.concatenate([share] * (WIDE // 128), axis=1)
+            outw[g, pl.ds(e * GSLOT, GSLOT), cols] = (
+                res[gi * GSLOT : (gi + 1) * GSLOT] * share
+            ).astype(jnp.bfloat16)
+
+    def spread(g, j):
+        cols = pl.ds(j * WIDE, WIDE)
+        ctr[pl.ds(g * GTOK, GTOK), cols] = jnp.dot(
+            st[g], outw[g, :, cols], preferred_element_type=jnp.float32
+        )
+
+    def cut(ref, source, h):
+        return ref.at[pl.ds(POS[source] * TOK, TOK), pl.ds(h * HALF, HALF)]
 
     def rs_wait(s, way, h):
-        buf = (rsr, rsl)[way].at[s - 1, pl.ds(h * SUB, SUB), :]
+        buf = (rsr, rsl)[way].at[s - 1, :, pl.ds(h * HALF, HALF)]
         at = (way * 8 + s - 1) * 2 + h
         arrived(buf, rssend.at[at], rsrecv.at[at], zr if way == 0 else zl)
         return buf
 
-    def rs(s):
-        for h in (0, 1):
-            for way in (0, 1):
-                if s == 0 and h != way:
-                    continue
-                source = 8 + s if way == 0 else 8 - s
-                total = mine(source, h)
-                if s > 1 or (s == 1 and h == way):
-                    total = total + rs_wait(s, way, h)[...].astype(jnp.float32)
-                blk = block(source, h)
-                blk[...] = total.astype(jnp.bfloat16)
-                at = (way * 8 + s) * 2 + h
-                dst = (rsr, rsl)[way].at[s, pl.ds(h * SUB, SUB), :]
-                send(blk, dst, rssend.at[at], rsrecv.at[at], zr if way == 0 else zl)
+    def rs(s, h):
+        for way in (0, 1):
+            if s == 0 and h != way:
+                continue
+            source = 8 + s if way == 0 else 8 - s
+            total = cut(ctr, source, h)[...]
+            if s > 1 or (s == 1 and h == way):
+                total = total + rs_wait(s, way, h)[...].astype(jnp.float32)
+            blk = cut(x_buf, source, h)
+            blk[...] = total.astype(jnp.bfloat16)
+            at = (way * 8 + s) * 2 + h
+            dst = (rsr, rsl)[way].at[s, :, pl.ds(h * HALF, HALF)]
+            send(blk, dst, rssend.at[at], rsrecv.at[at], zr if way == 0 else zl)
 
     route[0] = routing_ref[...]
     weights(0, 0)
@@ -483,15 +471,18 @@
     ag_start(0, 0)
     ag_start(0, 1)
     plan = [
-        ("ag", 0), ("ag", 1), ("ag", 2), ("ag", 3), ("w", 0, 2), ("ag", 4),
-        ("ag", 5), ("w", 0, 3), ("dispatch", 3), ("ag", 6), ("ag", 7), ("ag", 8), ("w", 0, 4), ("w", 1, 0),
-        ("ag", 9), ("dispatch", 2), ("w", 0, 5), ("ag", 10), ("ag", 11), ("w", 0, 6), ("ag", 12), ("dispatch", 1), ("w", 0, 7),
-        ("ag", 13), ("w", 1, 1), ("w", 0, 8), ("ag", 14), ("ag", 15), ("w", 1, 2), ("gate_up", 1, 0),
-        ("w", 1, 3), ("dispatch", 0), ("w", 1, 4), ("gate_up", 1, 1), ("w", 1, 5), ("w", 1, 6),
-        ("gate_up", 0, 0), ("w", 1, 7), ("gate_up", 0, 1), ("w", 1, 8), ("agdone",),
-        ("down", 0, 0), ("down", 0, 1), ("spread", 0), ("rs", 0), ("rs", 1), ("spread", 1), ("rs", 2),
-        ("down", 1, 0), ("rs", 3), ("down", 1, 1), ("spread", 2), ("rs", 4), ("spread", 3),
-        ("rs", 5), ("rs", 6), ("rs", 7),
+        "w02", "ag0", "w03", "ag1", "ag2", "w10", "ag3", "dispatch3", "ag4", "w04", "ag5", "w05",
+        "ag6", "ag7", "dispatch2", "w06", "ag8", "ag9", "w11", "w07", "ag10", "w12", "ag11", "w08",
+        "dispatch1", "ag12", "w13", "gate_up100", "gate_up101", "ag13", "gate_up102", "w14",
+        "gate_up103", "ag14", "gate_up110", "gate_up111", "ag15", "w15", "dispatch0", "gate_up112",
+        "w16", "gate_up113", "gate_up000", "gate_up001", "gate_up002", "w17", "gate_up003",
+        "gate_up010", "gate_up011", "gate_up012", "gate_up013", "w18", "agdone", "down000",
+        "down010", "down001", "down011", "spread00", "spread01", "rs00", "down002", "down012",
+        "down003", "down013", "spread02", "spread03", "rs01", "spread10", "spread11", "rs10",
+        "spread12", "spread13", "rs11", "down100", "down110", "rs20", "down101", "down111", "rs21",
+        "down102", "down112", "rs30", "down103", "down113", "rs31", "spread20", "spread21", "rs40",
+        "spread22", "spread23", "rs41", "spread30", "spread31", "rs50", "spread32", "spread33",
+        "rs51", "rs60", "rs61", "rs70", "rs71",
     ]
 
     def ag_done():
@@ -502,14 +493,17 @@
         "ag": ag, "w": weights, "dispatch": dispatch, "gate_up": gate_up, "down": down,
         "spread": spread, "rs": rs, "agdone": ag_done,
     }
-    for name, *args in plan:
-        run[name](*args)
+    for item in plan:
+        name = item.rstrip("0123456789")
+        digits = item[len(name) :]
+        run[name](*([int(digits)] if name == "ag" else [int(c) for c in digits]))
 
     for h in (0, 1):
-        total = resid_s[pl.ds(h * SUB, SUB), :].astype(jnp.float32) + mine(0, h)
+        cols = pl.ds(h * HALF, HALF)
+        total = resid_s[:, cols].astype(jnp.float32) + cut(ctr, 0, h)[...]
         for way in (0, 1):
             total = total + rs_wait(8, way, h)[...].astype(jnp.float32)
-        out_ref[pl.ds(h * SUB, SUB), :] = total.astype(jnp.bfloat16)
+        out_ref[:, cols] = total.astype(jnp.bfloat16)
     for copy in pending:
         copy.wait_send()
 

time: 158 us -> 143 us (0.905)
  Pallas kernels: 154 us -> 139 us
    pallas_call x1, Pallas kernels: 154 us -> 139 us  [moe(): pl.pallas_call(moe_kernel, out_shape=jax.ShapeDtypeStruct((TOK, D), bf),...]
where the time goes in v3:
time: 143 us
  Pallas kernels  139 us (97%)
  local copies, waits for them, and re-layouts  3.64 us (3%)
    pallas_call x1, Pallas kernels, moe(): pl.pallas_call(moe_kernel, out_shape=jax.ShapeDtypeStruct((TOK, D), bf),...  139 us
    unnamed x5, local copies, waits for them, and re-layouts  3.04 us

profile of v3, /device:TPU:1, one launch (start us, length us, event | category | flops | bytes accessed | tf_op | source)
XLA Modules:
  0.0 142.6 jit_solution(1142607085867839428)
XLA Ops:
  0.0 0.0 copy-start
  0.0 0.7 copy-done
  0.7 0.0 copy-start.1
  0.7 0.7 copy-done.1
  1.4 0.6 pad.4.routing_ref
  2.0 138.9 %shard_map.109 = bf16[64,2048]{1,0:T(8,128)(2,1)} custom-call(s32[1,8]{1,0:T(1,128)} %table_ref.1, s32[1,4]{1,0:T(1,128)} %length_ref.1, bf16[1024,128]{1,0:T(8,128)(2,1)} %bitcast.14, bf16[8,128,128]{2,1,0:T(8,128)(2,1)} %k_ref.1, bf16[8,128,128]{2,1,0:T(8,128)(2,1)} %v_ref.1, bf16[64,2048]{1,0:T(8,128)(2,1)} %bitcast.15, f32[1,2048]{1,0:T(1,128)} %bitcast.16, ...), custom_call_target="tpu_custom_call" | custom-call | tf_op jit(solution)/shard_map/pallas_call | solution.py:517
  140.9 1.7 %copy.13 = bf16[1,64,2048]{2,1,0:T(8,128)(2,1)} copy(bf16[1,64,2048]{2,1,0:T(8,128)(2,1)} %bitcast.12) | data formatting | bytes 524288
  (2 shorter events, 0.0 us)
Async XLA Ops:
  0.0 0.7 copy-start
  0.7 0.7 copy-start.1

commit v4 on v3

--- a/solution.py
+++ b/solution.py
@@ -33,7 +33,9 @@
 ORDER = (8, 7, 9, 6, 10, 5, 11, 4, 12, 3, 13, 2, 14, 1, 15, 0)
 POS = {s: i for i, s in enumerate(ORDER)}
 
-ROWS = (128, 64)
+ROWS = (128, 64, 64)
+COL0 = (0, 0, D // 2)
+COLS = (2 * FF, D // 2, D // 2)
 KS = (0, 1, -1, 2)
 NMSG = 4 + 4 * len(KS)
 
@@ -147,7 +149,7 @@
         rows = ROWS[stream]
         first = pl.multiple_of(((sx * 2 + sy // 2) * 2 + core) * rows + off, 16)
         buf = wd if stream else wg
-        return buf.at[sy % 2, pl.ds(first, n), :]
+        return buf.at[sy % 2, pl.ds(first, n), pl.ds(COL0[stream], COLS[stream])]
 
     def piece(stream, half, k1, k2, part):
         h = ROWS[stream] // 2
@@ -206,16 +208,21 @@
                 rows = ROWS[stream]
                 first = pl.multiple_of(((sx * 2 + sy // 2) * 2 + 1 - core) * rows, 16)
                 buf = wd if stream else wg
-                ref = buf.at[sy % 2, pl.ds(first, rows), :]
+                cols = pl.ds(COL0[stream], COLS[stream])
+                ref = buf.at[sy % 2, pl.ds(first, rows), cols]
                 arrived(ref, sibsend.at[at], sibrecv.at[at], sibling)
 
     def weights(stream, phase):
         if phase == 0:
-            (load_gu, load_dn)[stream].wait()
-            src = (gu32, dn32)[stream]
+            if stream < 2:
+                (load_gu, load_dn)[stream].wait()
+            src = (gu32, dn32, dn32)[stream]
+            cols = pl.ds(COL0[stream], COLS[stream])
             rows = ROWS[stream]
             first = pl.multiple_of(dp * rows, 16)
-            (wg, wd)[stream][y % 2, pl.ds(first, rows), :] = src[...].astype(jnp.bfloat16)
+            (wg, wd, wd)[stream][y % 2, pl.ds(first, rows), cols] = src[:, cols].astype(
+                jnp.bfloat16
+            )
             if stream == 0:
                 pl.semaphore_wait(barrier, len(partners))
             for index in (0, 1, p2(0, 0), p2(0, 1)):
@@ -341,7 +348,6 @@
         pick = jnp.concatenate(picks, axis=0)
         st[g] = pick.T.astype(jnp.bfloat16)
         pick = pick.astype(jnp.bfloat16)
-        b, gi = g // 2, g % 2
         for c in range(0, D, 512):
             rows = jnp.dot(
                 pick,
@@ -349,25 +355,31 @@
                 preferred_element_type=jnp.float32,
             ).astype(jnp.bfloat16)
             for e in (0, 1):
-                xs[b, e, pl.ds(gi * GSLOT, GSLOT), pl.ds(c, 512)] = rows[
+                xs[e, pl.ds(g * GSLOT, GSLOT), pl.ds(c, 512)] = rows[
                     e * GSLOT : (e + 1) * GSLOT
                 ]
 
+    def batch_rows(b):
+        return pl.ds(GSLOT, (NGRP - 1) * GSLOT) if b else pl.ds(0, GSLOT)
+
     def gate_up(b, e, j):
-        lhs = xs[b, e]
+        at = batch_rows(b)
+        lhs = xs[e, at, :]
         cols = pl.ds(j * 256, 256)
         gate = jnp.dot(lhs, wg[e, :, cols], preferred_element_type=jnp.float32)
         up = jnp.dot(
             lhs, wg[e, :, pl.ds(FF + j * 256, 256)], preferred_element_type=jnp.float32
         )
         hid = gate / (1.0 + jnp.exp(-gate)) * up
-        act[b, e, :, cols] = hid.astype(jnp.bfloat16)
+        act[e, at, cols] = hid.astype(jnp.bfloat16)
 
     def down(b, e, j):
         cols = pl.ds(j * WIDE, WIDE)
-        res = jnp.dot(act[b, e], wd[e, :, cols], preferred_element_type=jnp.float32)
-        for gi in (0, 1):
-            g = b * 2 + gi
+        res = jnp.dot(
+            act[e, batch_rows(b), :], wd[e, :, cols], preferred_element_type=jnp.float32
+        )
+        for gi in range(NGRP - 1 if b else 1):
+            g = b + gi
             share = wcol[g, pl.ds(e * GSLOT, GSLOT), :]
             share = jnp.concatenate([share] * (WIDE // 128), axis=1)
             outw[g, pl.ds(e * GSLOT, GSLOT), cols] = (
@@ -472,17 +484,18 @@
     ag_start(0, 1)
     plan = [
         "w02", "ag0", "w03", "ag1", "ag2", "w10", "ag3", "dispatch3", "ag4", "w04", "ag5", "w05",
-        "ag6", "ag7", "dispatch2", "w06", "ag8", "ag9", "w11", "w07", "ag10", "w12", "ag11", "w08",
-        "dispatch1", "ag12", "w13", "gate_up100", "gate_up101", "ag13", "gate_up102", "w14",
-        "gate_up103", "ag14", "gate_up110", "gate_up111", "ag15", "w15", "dispatch0", "gate_up112",
-        "w16", "gate_up113", "gate_up000", "gate_up001", "gate_up002", "w17", "gate_up003",
-        "gate_up010", "gate_up011", "gate_up012", "gate_up013", "w18", "agdone", "down000",
-        "down010", "down001", "down011", "spread00", "spread01", "rs00", "down002", "down012",
-        "down003", "down013", "spread02", "spread03", "rs01", "spread10", "spread11", "rs10",
-        "spread12", "spread13", "rs11", "down100", "down110", "rs20", "down101", "down111", "rs21",
-        "down102", "down112", "rs30", "down103", "down113", "rs31", "spread20", "spread21", "rs40",
-        "spread22", "spread23", "rs41", "spread30", "spread31", "rs50", "spread32", "spread33",
-        "rs51", "rs60", "rs61", "rs70", "rs71",
+        "ag6", "ag7", "dispatch2", "w06", "ag8", "w11", "ag9", "w20", "w07", "ag10", "w12", "ag11",
+        "w08", "dispatch1", "w13", "gate_up100", "ag12", "w14", "gate_up101", "w21", "gate_up102",
+        "ag13", "w22", "gate_up103", "w15", "gate_up110", "ag14", "w16", "gate_up111", "w23",
+        "gate_up112", "w17", "gate_up113", "ag15", "w24", "dispatch0", "gate_up000", "w18",
+        "gate_up001", "gate_up002", "w25", "gate_up003", "gate_up010", "w26", "gate_up011",
+        "gate_up012", "gate_up013", "agdone", "down000", "down010", "down001", "down011",
+        "spread00", "spread01", "rs00", "w27", "down100", "down110", "rs10", "down101", "down111",
+        "spread10", "spread11", "w28", "down002", "down012", "down003", "down013", "spread02",
+        "spread03", "rs01", "rs20", "down102", "down112", "rs11", "rs30", "down103", "down113",
+        "spread12", "spread13", "rs21", "spread20", "spread21", "rs40", "rs31", "spread22",
+        "spread23", "spread30", "spread31", "rs50", "rs41", "rs60", "spread32", "spread33", "rs51",
+        "rs70", "rs61", "rs71",
     ]
 
     def ag_done():
@@ -530,8 +543,8 @@
             pltpu.VMEM((2, FF, D), bf),
             pltpu.VMEM((ROWS[0], D), f32),
             pltpu.VMEM((ROWS[1], D), f32),
-            pltpu.VMEM((2, 2, 2 * GSLOT, D), bf),
-            pltpu.VMEM((2, 2, 2 * GSLOT, FF), bf),
+            pltpu.VMEM((2, NGRP * GSLOT, D), bf),
+            pltpu.VMEM((2, NGRP * GSLOT, FF), bf),
             pltpu.VMEM((NGRP, 2 * GSLOT, D), bf),
             pltpu.VMEM((NGRP, 2 * GSLOT, 128), f32),
             pltpu.VMEM((NGRP, GTOK, 2 * GSLOT), bf),
@@ -540,10 +553,10 @@
             pltpu.VMEM((8, TOK, D), bf),
             pltpu.VMEM((TOK, D), bf),
             dma((2,)),
-            dma((4 * NMSG,)),
-            dma((4 * NMSG,)),
-            dma((32,)),
-            dma((32,)),
+            dma((6 * NMSG,)),
+            dma((6 * NMSG,)),
+            dma((48,)),
+            dma((48,)),
             dma((32,)),
             dma((32,)),
             dma((32,)),

time: 143 us -> 148 us (1.035)
  Pallas kernels: 139 us -> 144 us
    pallas_call x1, Pallas kernels: 139 us -> 144 us  [moe(): pl.pallas_call(moe_kernel, out_shape=jax.ShapeDtypeStruct((TOK, D), bf),...]
where the time goes in v4:
time: 148 us; the launch traced here: 147 us
  Pallas kernels  144 us (97%)
  local copies, waits for them, and re-layouts  3.64 us (2%)
    pallas_call x1, Pallas kernels, moe(): pl.pallas_call(moe_kernel, out_shape=jax.ShapeDtypeStruct((TOK, D), bf),...  144 us
    unnamed x5, local copies, waits for them, and re-layouts  3.04 us

profile of v4, /device:TPU:1, one launch (start us, length us, event | category | flops | bytes accessed | tf_op | source)
XLA Modules:
  0.0 147.4 jit_solution(5752864769261017056)
XLA Ops:
  0.0 0.0 copy-start
  0.0 0.7 copy-done
  0.7 0.0 copy-start.1
  0.7 0.7 copy-done.1
  1.4 0.6 pad.4.routing_ref
  2.0 143.7 %shard_map.109 = bf16[64,2048]{1,0:T(8,128)(2,1)} custom-call(s32[1,8]{1,0:T(1,128)} %table_ref.1, s32[1,4]{1,0:T(1,128)} %length_ref.1, bf16[1024,128]{1,0:T(8,128)(2,1)} %bitcast.14, bf16[8,128,128]{2,1,0:T(8,128)(2,1)} %k_ref.1, bf16[8,128,128]{2,1,0:T(8,128)(2,1)} %v_ref.1, bf16[64,2048]{1,0:T(8,128)(2,1)} %bitcast.15, f32[1,2048]{1,0:T(1,128)} %bitcast.16, ...), custom_call_target="tpu_custom_call" | custom-call | tf_op jit(solution)/shard_map/pallas_call | solution.py:530
  145.7 1.7 %copy.13 = bf16[1,64,2048]{2,1,0:T(8,128)(2,1)} copy(bf16[1,64,2048]{2,1,0:T(8,128)(2,1)} %bitcast.12) | data formatting | bytes 524288
  (2 shorter events, 0.0 us)
Async XLA Ops:
  0.0 0.7 copy-start
  0.7 0.7 copy-start.1

commit v5 on v3

--- a/solution.py
+++ b/solution.py
@@ -41,15 +41,20 @@
 def moe_kernel(
     table_ref,
     length_ref,
+    q_hbm,
+    k_hbm,
+    v_hbm,
+    hidden_hbm,
+    gain_ref,
+    ids_ref,
+    gates_ref,
+    gu_hbm,
+    dn_hbm,
+    out_ref,
     q_ref,
     k_ref,
     v_ref,
     hidden_ref,
-    gain_ref,
-    routing_ref,
-    gu_hbm,
-    dn_hbm,
-    out_ref,
     keys,
     values,
     heads_out,
@@ -108,7 +113,15 @@
 
     load_gu = pltpu.make_async_copy(gu_hbm, gu32, load_sem.at[0])
     load_dn = pltpu.make_async_copy(dn_hbm, dn32, load_sem.at[1])
+    inputs = [
+        pltpu.make_async_copy(src, dst, load_sem.at[2 + i])
+        for i, (src, dst) in enumerate(
+            [(k_hbm, k_ref), (v_hbm, v_ref), (q_hbm, q_ref), (hidden_hbm, hidden_ref)]
+        )
+    ]
     load_gu.start()
+    for copy in inputs:
+        copy.start()
     load_dn.start()
 
     barrier = pltpu.get_barrier_semaphore()
@@ -403,9 +416,13 @@
             dst = (rsr, rsl)[way].at[s, :, pl.ds(h * HALF, HALF)]
             send(blk, dst, rssend.at[at], rsrecv.at[at], zr if way == 0 else zl)
 
-    route[0] = routing_ref[...]
+    route[0] = jnp.zeros((2 * TOPK, 2 * TOK), jnp.float32)
+    route[0, pl.ds(0, TOPK), pl.ds(0, TOK)] = ids_ref[...].astype(jnp.float32)
+    route[0, pl.ds(TOPK, TOPK), pl.ds(0, TOK)] = gates_ref[...]
     weights(0, 0)
 
+    for copy in inputs:
+        copy.wait()
     for p in range(PAGES):
         at = table_ref[0, p]
         keys[pl.ds(p * PAGE, PAGE), :] = k_ref[at]
@@ -508,7 +525,7 @@
         copy.wait_send()
 
 
-def moe(table, lengths, queries, keys, values, hidden, gain, routing, gate_up, down):
+def moe(table, lengths, queries, keys, values, hidden, gain, ids, gates, gate_up, down):
     vmem = pl.BlockSpec(memory_space=pltpu.VMEM)
     smem = pl.BlockSpec(memory_space=pltpu.SMEM)
     hbm = pl.BlockSpec(memory_space=pl.ANY)
@@ -517,9 +534,13 @@
     return pl.pallas_call(
         moe_kernel,
         out_shape=jax.ShapeDtypeStruct((TOK, D), bf),
-        in_specs=[smem] * 2 + [vmem] * 6 + [hbm] * 2,
+        in_specs=[smem] * 2 + [hbm] * 4 + [vmem] * 3 + [hbm] * 2,
         out_specs=vmem,
         scratch_shapes=[
+            pltpu.VMEM((COL, HDIM), bf),
+            pltpu.VMEM((PAGES, PAGE, HDIM), bf),
+            pltpu.VMEM((PAGES, PAGE, HDIM), bf),
+            pltpu.VMEM((TOK, D), bf),
             pltpu.VMEM((COL, HDIM), bf),
             pltpu.VMEM((COL, HDIM), bf),
             pltpu.VMEM((COL, HDIM), bf),
@@ -539,7 +560,7 @@
             pltpu.VMEM((8, TOK, D), bf),
             pltpu.VMEM((8, TOK, D), bf),
             pltpu.VMEM((TOK, D), bf),
-            dma((2,)),
+            dma((6,)),
             dma((4 * NMSG,)),
             dma((4 * NMSG,)),
             dma((32,)),
@@ -556,7 +577,7 @@
         compiler_params=pltpu.CompilerParams(
             collective_id=0, has_side_effects=True, vmem_limit_bytes=56 * 1024 * 1024
         ),
-    )(table, lengths, queries, keys, values, hidden, gain, routing, gate_up, down)
+    )(table, lengths, queries, keys, values, hidden, gain, ids, gates, gate_up, down)
 
 
 def local(
@@ -572,8 +593,6 @@
     trainer_gate_up,
     trainer_down,
 ):
-    routing = jnp.concatenate([expert_ids[0].astype(jnp.float32), gate_weights[0]], axis=1)
-    routing = jnp.pad(routing.T, ((0, 0), (0, TOK)))
     mixed = moe(
         page_table,
         prompt_lengths,
@@ -582,7 +601,8 @@
         value_pool,
         hidden_in[0],
         norm_gain[None],
-        routing,
+        expert_ids[0].T,
+        gate_weights[0].T,
         trainer_gate_up[0],
         trainer_down[0],
     )

time: 143 us -> 140 us (0.979)
  local copies, waits for them, and re-layouts: 3.64 us -> 1.67 us
    unnamed x5 -> x1, local copies, waits for them, and re-layouts: 3.04 us -> 1.67 us
where the time goes in v5:
time: 140 us
  Pallas kernels  139 us (99%)
  local copies, waits for them, and re-layouts  1.67 us (1%)
    pallas_call x1, Pallas kernels, moe(): pl.pallas_call(moe_kernel, out_shape=jax.ShapeDtypeStruct((TOK, D), bf),...  139 us

profile of v5, /device:TPU:1, one launch (start us, length us, event | category | flops | bytes accessed | tf_op | source)
XLA Modules:
  0.0 140.3 jit_solution(11805508659399175883)
XLA Ops:
  0.0 138.6 %shard_map.109 = bf16[64,2048]{1,0:T(8,128)(2,1)} custom-call(s32[1,8]{1,0:T(1,128)} %table_ref.1, s32[1,4]{1,0:T(1,128)} %length_ref.1, bf16[1024,128]{1,0:T(8,128)(2,1)} %bitcast.15, bf16[8,128,128]{2,1,0:T(8,128)(2,1)} %k_hbm.1, bf16[8,128,128]{2,1,0:T(8,128)(2,1)} %v_hbm.1, bf16[64,2048]{1,0:T(8,128)(2,1)} %bitcast.16, f32[1,2048]{1,0:T(1,128)} %bitcast.17, ...), custom_call_target="tpu_custom_call" | custom-call | tf_op jit(solution)/shard_map/pallas_call | solution.py:534
  138.6 1.7 %copy.13 = bf16[1,64,2048]{2,1,0:T(8,128)(2,1)} copy(bf16[1,64,2048]{2,1,0:T(8,128)(2,1)} %bitcast.13) | data formatting | bytes 524288
